TPU v7x, 32 devices: a whole 2x2x4 slice. The times are simulated.
32 devices in a mesh: pt: 8 (over z, y), tm: 4 (over x, core).
Axes of the slice: x: 2, y: 2, z: 4, core: 2. Of those that a mesh axis runs over, the one named last changes fastest.
Arguments:
- signals: float32 [512, 32768], P('pt', 'tm'), may hold values from -6 to 6
- freq_bins: int32 [4], replicated, may hold values from 1 to 511
Outputs:
- cross_spectra: float32 [2, 4, 512, 512], P(None, None, 'pt', 'tm')
All inputs are finite; a program needn't handle non-finite values.
Results may differ from a plain program's by a relative error of at most 0.000064.
Values sent between devices are 32-bit elements; how exact they have to be, the bound alone decides.
No kernel may reach another device: no remote copies, remote signals or barrier semaphores. Data moves between devices by JAX's collectives and lax.ppermute only.
A program may use at most 64 MiB of HBM per device.

v0:
```python
import math
import jax
import jax.numpy as jnp
from jax import lax
from jax.sharding import PartitionSpec as P

SEGLEN = 1024
TWO_PI = 2.0 * math.pi


def shifted(value, axis, steps):
    count = lax.axis_size(axis)
    initial, last = (max(0, -steps), min(count, count - steps))
    return lax.ppermute(value, axis, [(source, source + steps) for source in range(initial, last)])


def dft_tables(freq_bins, seg_len):
    sample_index = jnp.arange(seg_len, dtype=jnp.int32)
    wrapped = sample_index[:, None] * freq_bins[None, :] % seg_len
    angles = wrapped.astype(jnp.float32) * (TWO_PI / seg_len)
    window = 0.5 - 0.5 * jnp.cos(sample_index.astype(jnp.float32) * (TWO_PI / seg_len))
    cosine = window[:, None] * jnp.cos(angles)
    sine_part = -window[:, None] * jnp.sin(angles)
    full_table = jnp.concatenate([cosine, sine_part], axis=1)
    half_len = seg_len // 2
    return jnp.concatenate([full_table[:half_len], full_table[half_len:]], axis=1)


def tile_products(left_side, right_side):
    stacked_right = jnp.concatenate([right_side[:, 0], right_side[:, 1]], axis=2)
    real_left = jnp.concatenate([left_side[:, 0], left_side[:, 1]], axis=2)
    imag_left = jnp.concatenate([left_side[:, 1], -left_side[:, 0]], axis=2)
    real_part = jnp.einsum(
        "fps,fqs->fpq", real_left, stacked_right, precision=lax.Precision.HIGHEST
    )
    imag_part = jnp.einsum(
        "fps,fqs->fpq", imag_left, stacked_right, precision=lax.Precision.HIGHEST
    )
    return jnp.stack([real_part, imag_part])


def body(signals, freq_bins):
    point_rows, sample_count = signals.shape
    half_len = SEGLEN // 2
    blocks_dev = sample_count // half_len
    bin_count = freq_bins.shape[0]
    columns = 2 * bin_count
    table = dft_tables(freq_bins, SEGLEN)
    blocks = signals.reshape(point_rows, blocks_dev, half_len)
    projected = jnp.einsum("pbn,nc->pbc", blocks, table, precision=lax.Precision.HIGHEST)
    incoming = shifted(signals[:, :half_len], "tm", -1)
    boundary = jnp.dot(
        incoming,
        table[:, columns:],
        precision=lax.Precision.HIGHEST,
        preferred_element_type=jnp.float32,
    )
    following = jnp.concatenate([projected[:, 1:, columns:], boundary[:, None, :]], axis=1)
    spectra = projected[:, :, :columns] + following
    is_last = lax.axis_index("tm") == lax.axis_size("tm") - 1
    segment_ids = jnp.arange(blocks_dev, dtype=jnp.int32)
    weight_mask = jnp.where(
        jnp.logical_and(is_last, segment_ids == blocks_dev - 1), 0.0, 1.0
    ).astype(jnp.float32)
    spectra = spectra * weight_mask[None, :, None]
    spectra_panel = spectra.reshape(point_rows, blocks_dev, 2, bin_count).transpose(3, 2, 0, 1)
    partial_tiles = tile_products(
        spectra_panel, lax.all_gather(spectra_panel, "pt", axis=2, tiled=True)
    )
    summed = lax.psum_scatter(partial_tiles, "tm", scatter_dimension=3, tiled=True)
    total_segments = blocks_dev * lax.axis_size("tm") - 1
    scale = 1.0 / (total_segments * 0.375 * SEGLEN)
    return summed * scale


def solution(mesh):
    in_specs = (P("pt", "tm"), P())
    out_specs = P(None, None, "pt", "tm")
    return jax.shard_map(body, mesh=mesh, in_specs=in_specs, out_specs=out_specs, check_vma=False)
```

profile of v0, /device:TPU:0, one launch (start us, length us, event | category | flops | bytes accessed | tf_op | source)
XLA Modules:
  0.0 97.8 jit_solution(1529557021851676892)
XLA Ops:
  6.5 0.0 reduce-scatter.2.cloned.1.call-start
  6.5 0.9 slice.33
  7.5 1.3 %collective-permute-start = (f32[64,512]{1,0:T(8,128)S(1)}, f32[64,512]{1,0:T(8,128)S(1)}, u32[]{:S(2)}, u32[]{:S(2)}) collective-permute-start(f32[64,512]{1,0:T(8,128)S(1)} %slice.33), channel_id=1, source_target_pairs={{1,0},{2,1},{3,2},{5,4},{6,5},{7,6},{9,8},{10,9},{11,10},{13,12},{... | collective-permute-start | bytes 393224 | tf_op jit(solution)/shard_map/ppermute | solution.py:14
  8.8 0.9 cosine_multiply_fusion
  9.7 4.2 %fusion.3 = f32[64,16,16]{0,2,1:T(8,128)S(1)} fusion(f32[8,16,8,512]{3,2,1,0:T(8,128)} %bitcast.33, f32[512,8]{0,1:T(8,128)S(1)} %get-tuple-element.10, f32[512,8]{0,1:T(8,128)S(1)} %get-tuple-element.9), kind=kOutput, calls=%fused_computation.5 | convolution fusion | flops 100671488 | bytes 2195456 | tf_op jit(solution)/shard_map/pbn,nc->pbc/dot_general | solution.py:50
  13.9 0.0 collective-permute-done
  13.9 0.2 convolution_bitcast_fusion.2
  14.1 0.1 fusion.6
  14.2 0.2 copy.7
  14.4 47.1 %all_gather.3 = f32[4,2,512,16]{3,0,1,2:T(4,128)S(1)} all-gather(f32[4,2,64,16]{3,0,1,2:T(4,128)S(1)} %copy.7), channel_id=1, replica_groups=mesh['pt'=8,'tm'=4] {'pt'}, dimensions={2}, use_global_device_ids=true | all-gather | bytes 294912 | tf_op jit(solution)/shard_map/all_gather | solution.py:68
  61.5 0.4 fusion.24
  61.9 0.3 copy.10
  62.2 0.3 copy.11
  62.5 0.6 convolution_bitcast_fusion.1
  63.2 0.6 convolution_bitcast_fusion
  63.8 1.0 %pad_maximum_fusion = f32[2,4,64,512]{3,2,1,0:T(8,128)} fusion(f32[1,4,64,512]{3,2,1,0:T(8,128)S(1)} %convolution_bitcast_fusion, f32[1,4,64,512]{3,2,1,0:T(8,128)S(1)} %convolution_bitcast_fusion.1), kind=kLoop, calls=%fused_computation.7 | loop fusion | flops 262144 | bytes 2097152 | tf_op jit(solution)/shard_map/stack | solution.py:39
  64.9 0.0 reduce-scatter.2.cloned.1.call-update
  64.9 24.3 %reduce-scatter.2.cloned.1.call-done = f32[2,4,64,128]{3,2,1,0:T(8,128)} async-done(((f32[2,4,64,512]{3,2,1,0:T(8,128)}), f32[2,4,64,128]{3,2,1,0:T(8,128)}) %reduce-scatter.2.cloned.1.call-update) | async-done | bytes 262160 | tf_op jit(solution)/shard_map/reduce_scatter | solution.py:70
  89.2 1.7 %broadcast_multiply_fusion = f32[2,4,64,128]{3,2,1,0:T(8,128)} fusion(f32[2,4,64,128]{3,2,1,0:T(8,128)} %reduce-scatter.2.cloned.1.call-done), kind=kLoop, calls=%fused_computation.9 | loop fusion | flops 65536 | bytes 524288 | tf_op jit(solution)/shard_map/mul | solution.py:73
  (7 shorter events, 0.1 us)
Async XLA Ops:
  6.5 82.7 %reduce-scatter.2.cloned.1.call-start = ((), (), s32[]{:S(2)}) async-start(), calls=%async_computation.1 | async-start | bytes 1310720 | tf_op jit(solution)/shard_map/reduce_scatter | solution.py:70
  7.5 6.4 %collective-permute-start = (f32[64,512]{1,0:T(8,128)S(1)}, f32[64,512]{1,0:T(8,128)S(1)}, u32[]{:S(2)}, u32[]{:S(2)}) collective-permute-start(f32[64,512]{1,0:T(8,128)S(1)} %slice.33), channel_id=1, source_target_pairs={{1,0},{2,1},{3,2},{5,4},{6,5},{7,6},{9,8},{10,9},{11,10},{13,12},{... | collective-permute-start | bytes 393224 | tf_op jit(solution)/shard_map/ppermute | solution.py:14
Sparse Core Ops, SparseCore 0:
  65.0 24.1 reduce-scatter.1
where the time goes:
time: 98 us; the launch traced here: 97.8 us
  blocking collectives  47.1 us (48%)
  waiting for transfers between devices  24.4 us (25%)
  between operations  13.5 us (14%)
  matrix products  5.6 us (6%)
  other arithmetic  3.79 us (4%)
  local copies, waits for them, and re-layouts  2.13 us (2%)
  starting transfers between devices  1.29 us (1%)
    all_gather x1, blocking collectives, body(): lax.all_gather(spectra_panel, 'pt', axis=2, tiled=True)  47.1 us
    reduce_scatter x1, waiting for transfers between devices, body(): lax.psum_scatter(partial_tiles, 'tm', scatter_dimension=3, tiled=True)  24.3 us
    dot_general x1, matrix products, body(): jnp.einsum('pbn,nc->pbc', blocks, table, precision=lax.Precision.HIGHEST)  4.15 us
  transfers between devices with their start and end apart: 2, of which 1 were waited for; matrix products, arithmetic and copies ran while one was open for 5% of the time, Pallas kernels for 0%

commit v1 on v0

--- a/solution.py
+++ b/solution.py
@@ -40,6 +40,29 @@
 
 
 def body(signals, freq_bins):
+
+    def _do_loads(xs):
+        q_n = jax.lax.psum(1, "pt")
+        g_now = range(q_n)
+        t_next = map(lambda it: (it, (it + 1) % q_n), g_now)
+        views = list(t_next)
+        wide_out = range(q_n)
+        everything = map(lambda it: (it, (it - 1) % q_n), wide_out)
+        column = list(everything)
+        new, base_arr = ([xs], [xs])
+        for _ in range(q_n // 2):
+            local_next = jax.lax.ppermute(new[-1], "pt", views)
+            new.append(local_next)
+        c = 0
+        while c < (q_n - 1) // 2:
+            earlier = jax.lax.ppermute(base_arr[-1], "pt", column)
+            base_arr.append(earlier)
+            c = c + 1
+        x_new = jnp.concatenate([*new[::-1], *base_arr[1:]], 2)
+        low = jax.lax.axis_index("pt")
+        n_now = jnp.roll(x_new, (low - q_n // 2) * xs.shape[2], axis=2)
+        return n_now
+
     point_rows, sample_count = signals.shape
     half_len = SEGLEN // 2
     blocks_dev = sample_count // half_len
@@ -64,9 +87,7 @@
     ).astype(jnp.float32)
     spectra = spectra * weight_mask[None, :, None]
     spectra_panel = spectra.reshape(point_rows, blocks_dev, 2, bin_count).transpose(3, 2, 0, 1)
-    partial_tiles = tile_products(
-        spectra_panel, lax.all_gather(spectra_panel, "pt", axis=2, tiled=True)
-    )
+    partial_tiles = tile_products(spectra_panel, _do_loads(spectra_panel))
     summed = lax.psum_scatter(partial_tiles, "tm", scatter_dimension=3, tiled=True)
     total_segments = blocks_dev * lax.axis_size("tm") - 1
     scale = 1.0 / (total_segments * 0.375 * SEGLEN)

time: 98 us -> 78.4 us (0.80)
  blocking collectives: 47.1 us -> 0 us
  starting transfers between devices: 1.29 us -> 16.7 us
  waiting for transfers between devices: 24.4 us -> 37.2 us
    all_gather x1 -> x0, blocking collectives: 47.1 us -> none  [body(): lax.all_gather(spectra_panel, 'pt', axis=2, tiled=True)]
    ppermute x0 -> x7, starting transfers between devices: none -> 15.4 us  [the longest x3 12.4 us: _do_loads(): earlier = jax.lax.ppermute(base_arr[-1], 'pt', column)]
    ppermute x0 -> x7, waiting for transfers between devices: none -> 14.2 us  [the longest x4 13.7 us: _do_loads(): local_next = jax.lax.ppermute(new[-1], 'pt', views)]
    reduce_scatter x1, waiting for transfers between devices: 24.3 us -> 23 us  [body(): lax.psum_scatter(partial_tiles, 'tm', scatter_dimension=3, tiled=True)]
  transfers between devices with their start and end apart: 2 -> 9, of which waited for: 1 -> 6; matrix products, arithmetic and copies ran while one was open for 5% -> 7% of each run, Pallas kernels for 0% -> 0%
where the time goes in v1:
time: 78.4 us; the launch traced here: 78.2 us
  waiting for transfers between devices  37.2 us (47%)
  starting transfers between devices  16.7 us (21%)
  between operations  13.5 us (17%)
  matrix products  5.59 us (7%)
  other arithmetic  3.79 us (5%)
  local copies, waits for them, and re-layouts  1.36 us (2%)
    reduce_scatter x1, waiting for transfers between devices, body(): lax.psum_scatter(partial_tiles, 'tm', scatter_dimension=3, tiled=True)  23 us
    ppermute x4, waiting for transfers between devices, _do_loads(): local_next = jax.lax.ppermute(new[-1], 'pt', views)  13.7 us
    ppermute x3, starting transfers between devices, _do_loads(): earlier = jax.lax.ppermute(base_arr[-1], 'pt', column)  12.4 us
    dot_general x1, matrix products, body(): jnp.einsum('pbn,nc->pbc', blocks, table, precision=lax.Precision.HIGHEST)  4.15 us
    ppermute x4, starting transfers between devices, _do_loads(): local_next = jax.lax.ppermute(new[-1], 'pt', views)  3.03 us
    mul x1, other arithmetic, body(): return summed * scale  1.68 us
  transfers between devices with their start and end apart: 9, of which 6 were waited for; matrix products, arithmetic and copies ran while one was open for 7% of the time, Pallas kernels for 0%

profile of v1, /device:TPU:0, one launch (start us, length us, event | category | flops | bytes accessed | tf_op | source)
XLA Modules:
  0.0 78.2 jit_solution(13676473897289106559)
XLA Ops:
  6.5 0.0 reduce-scatter.2.cloned.1.call-start
  6.5 0.9 %slice.33 = f32[64,512]{1,0:T(8,128)S(1)} slice(f32[64,8192]{1,0:T(8,128)} %param.2), slice={[0:64], [0:512]} | slice | bytes 262144 | tf_op jit(solution)/shard_map/slice | solution.py:74
  7.5 1.3 %collective-permute-start = (f32[64,512]{1,0:T(8,128)S(1)}, f32[64,512]{1,0:T(8,128)S(1)}, u32[]{:S(2)}, u32[]{:S(2)}) collective-permute-start(f32[64,512]{1,0:T(8,128)S(1)} %slice.33), channel_id=1, source_target_pairs={{1,0},{2,1},{3,2},{5,4},{6,5},{7,6},{9,8},{10,9},{11,10},{13,12},{... | collective-permute-start | bytes 393224 | tf_op jit(solution)/shard_map/ppermute | solution.py:14
  8.8 0.9 %cosine_multiply_fusion = (f32[1024,4]{0,1:T(4,128)S(1)}, f32[1024,4]{0,1:T(4,128)S(1)}) fusion(s32[4]{0:T(128)} %param.3, f32[1024]{0:T(1024)S(1)} %get-tuple-element.13, f32[1024]{0:T(1024)S(1)} %get-tuple-element.14), kind=kLoop, calls=%fused_computation.37 | loop fusion | flops 65536 | bytes 40976 | tf_op jit(solution)/shard_map/mul | solution.py:22
  9.7 4.2 %fusion.3 = f32[64,16,16]{0,2,1:T(8,128)S(1)} fusion(f32[8,16,8,512]{3,2,1,0:T(8,128)} %bitcast.35, f32[512,8]{0,1:T(8,128)S(1)} %get-tuple-element.10, f32[512,8]{0,1:T(8,128)S(1)} %get-tuple-element.9), kind=kOutput, calls=%fused_computation.5 | convolution fusion | flops 100671488 | bytes 2195456 | tf_op jit(solution)/shard_map/pbn,nc->pbc/dot_general | solution.py:73
  13.9 0.0 collective-permute-done
  13.9 0.2 convolution_bitcast_fusion.2
  14.1 0.1 fusion.6
  14.2 3.0 %collective-permute-start.1 = (f32[4,2,64,16]{2,3,0,1:T(8,128)S(1)}, f32[4,2,64,16]{2,3,0,1:T(8,128)S(1)}, u32[]{:S(2)}, u32[]{:S(2)}) collective-permute-start(f32[4,2,64,16]{2,3,0,1:T(8,128)S(1)} %bitcast.36), channel_id=1, source_target_pairs={{0,4},{4,8},{8,12},{12,16},{16,20},{20,24},{24,28},{28,0},{1,5},{5... | collective-permute-start | bytes 98312 | tf_op jit(solution)/shard_map/ppermute | solution.py:54
  17.3 3.1 %collective-permute-start.5 = (f32[4,2,64,16]{2,3,0,1:T(8,128)S(1)}, f32[4,2,64,16]{2,3,0,1:T(8,128)S(1)}, u32[]{:S(2)}, u32[]{:S(2)}) collective-permute-start(f32[4,2,64,16]{2,3,0,1:T(8,128)S(1)} %bitcast.37), channel_id=1, source_target_pairs={{0,28},{4,0},{8,4},{12,8},{16,12},{20,16},{24,20},{28,24},{1,29},{... | collective-permute-start | bytes 98312 | tf_op jit(solution)/shard_map/ppermute | solution.py:58
  20.4 2.6 %collective-permute-done.1 = f32[4,2,64,16]{2,3,0,1:T(8,128)S(1)} collective-permute-done((f32[4,2,64,16]{2,3,0,1:T(8,128)S(1)}, f32[4,2,64,16]{2,3,0,1:T(8,128)S(1)}, u32[]{:S(2)}, u32[]{:S(2)}) %collective-permute-start.1) | collective-permute-done | bytes 32800 | tf_op jit(solution)/shard_map/ppermute | solution.py:54
  23.0 0.0 collective-permute-start.2
  23.0 0.5 collective-permute-done.5
  23.5 4.4 %collective-permute-start.6 = (f32[4,2,64,16]{2,3,0,1:T(8,128)S(1)}, f32[4,2,64,16]{2,3,0,1:T(8,128)S(1)}, u32[]{:S(2)}, u32[]{:S(2)}) collective-permute-start(f32[4,2,64,16]{2,3,0,1:T(8,128)S(1)} %collective-permute-done.5), channel_id=1, source_target_pairs={{0,28},{4,0},{8,4},{12,8},{16,12},{20,16},{24,20},{28,24},{1,29},{... | collective-permute-start | bytes 98312 | tf_op jit(solution)/shard_map/ppermute | solution.py:58
  27.9 2.1 %collective-permute-done.2 = f32[4,2,64,16]{2,3,0,1:T(8,128)S(1)} collective-permute-done((f32[4,2,64,16]{2,3,0,1:T(8,128)S(1)}, f32[4,2,64,16]{2,3,0,1:T(8,128)S(1)}, u32[]{:S(2)}, u32[]{:S(2)}) %collective-permute-start.2) | collective-permute-done | bytes 32800 | tf_op jit(solution)/shard_map/ppermute | solution.py:54
  29.9 0.0 collective-permute-start.3
  30.0 0.0 collective-permute-done.6
  30.0 4.9 %collective-permute-start.7 = (f32[4,2,64,16]{2,3,0,1:T(8,128)S(1)}, f32[4,2,64,16]{2,3,0,1:T(8,128)S(1)}, u32[]{:S(2)}, u32[]{:S(2)}) collective-permute-start(f32[4,2,64,16]{2,3,0,1:T(8,128)S(1)} %collective-permute-done.6), channel_id=1, source_target_pairs={{0,28},{4,0},{8,4},{12,8},{16,12},{20,16},{24,20},{28,24},{1,29},{... | collective-permute-start | bytes 98312 | tf_op jit(solution)/shard_map/ppermute | solution.py:58
  34.9 2.0 %collective-permute-done.3 = f32[4,2,64,16]{2,3,0,1:T(8,128)S(1)} collective-permute-done((f32[4,2,64,16]{2,3,0,1:T(8,128)S(1)}, f32[4,2,64,16]{2,3,0,1:T(8,128)S(1)}, u32[]{:S(2)}, u32[]{:S(2)}) %collective-permute-start.3) | collective-permute-done | bytes 32800 | tf_op jit(solution)/shard_map/ppermute | solution.py:54
  36.9 0.0 collective-permute-start.4
  36.9 0.0 collective-permute-done.7
  36.9 6.9 %collective-permute-done.4 = f32[4,2,64,16]{2,3,0,1:T(8,128)S(1)} collective-permute-done((f32[4,2,64,16]{2,3,0,1:T(8,128)S(1)}, f32[4,2,64,16]{2,3,0,1:T(8,128)S(1)}, u32[]{:S(2)}, u32[]{:S(2)}) %collective-permute-start.4) | collective-permute-done | bytes 32800 | tf_op jit(solution)/shard_map/ppermute | solution.py:54
  43.9 0.3 concatenate.28
  44.2 0.1 dynamic-slice_bitcast_fusion.1
  44.3 0.6 convolution_bitcast_fusion
  44.9 0.6 convolution_bitcast_fusion.1
  45.6 1.0 %pad_maximum_fusion = f32[2,4,64,512]{3,2,1,0:T(8,128)} fusion(f32[1,4,64,512]{3,2,1,0:T(8,128)S(1)} %convolution_bitcast_fusion, f32[1,4,64,512]{3,2,1,0:T(8,128)S(1)} %convolution_bitcast_fusion.1), kind=kLoop, calls=%fused_computation.7 | loop fusion | flops 262144 | bytes 2097152 | tf_op jit(solution)/shard_map/stack | solution.py:39
  46.6 0.0 reduce-scatter.2.cloned.1.call-update
  46.6 23.0 %reduce-scatter.2.cloned.1.call-done = f32[2,4,64,128]{3,2,1,0:T(8,128)} async-done(((f32[2,4,64,512]{3,2,1,0:T(8,128)}), f32[2,4,64,128]{3,2,1,0:T(8,128)}) %reduce-scatter.2.cloned.1.call-update) | async-done | bytes 262160 | tf_op jit(solution)/shard_map/reduce_scatter | solution.py:91
  69.6 1.7 %broadcast_multiply_fusion = f32[2,4,64,128]{3,2,1,0:T(8,128)} fusion(f32[2,4,64,128]{3,2,1,0:T(8,128)} %reduce-scatter.2.cloned.1.call-done), kind=kLoop, calls=%fused_computation.11 | loop fusion | flops 65536 | bytes 524288 | tf_op jit(solution)/shard_map/mul | solution.py:94
  (7 shorter events, 0.1 us)
Async XLA Ops:
  6.5 63.1 %reduce-scatter.2.cloned.1.call-start = ((), (), s32[]{:S(2)}) async-start(), calls=%async_computation.1 | async-start | bytes 1310720 | tf_op jit(solution)/shard_map/reduce_scatter | solution.py:91
  7.5 6.4 %collective-permute-start = (f32[64,512]{1,0:T(8,128)S(1)}, f32[64,512]{1,0:T(8,128)S(1)}, u32[]{:S(2)}, u32[]{:S(2)}) collective-permute-start(f32[64,512]{1,0:T(8,128)S(1)} %slice.33), channel_id=1, source_target_pairs={{1,0},{2,1},{3,2},{5,4},{6,5},{7,6},{9,8},{10,9},{11,10},{13,12},{... | collective-permute-start | bytes 393224 | tf_op jit(solution)/shard_map/ppermute | solution.py:14
  14.2 8.7 %collective-permute-start.1 = (f32[4,2,64,16]{2,3,0,1:T(8,128)S(1)}, f32[4,2,64,16]{2,3,0,1:T(8,128)S(1)}, u32[]{:S(2)}, u32[]{:S(2)}) collective-permute-start(f32[4,2,64,16]{2,3,0,1:T(8,128)S(1)} %bitcast.36), channel_id=1, source_target_pairs={{0,4},{4,8},{8,12},{12,16},{16,20},{20,24},{24,28},{28,0},{1,5},{5... | collective-permute-start | bytes 98312 | tf_op jit(solution)/shard_map/ppermute | solution.py:54
  17.3 6.2 %collective-permute-start.5 = (f32[4,2,64,16]{2,3,0,1:T(8,128)S(1)}, f32[4,2,64,16]{2,3,0,1:T(8,128)S(1)}, u32[]{:S(2)}, u32[]{:S(2)}) collective-permute-start(f32[4,2,64,16]{2,3,0,1:T(8,128)S(1)} %bitcast.37), channel_id=1, source_target_pairs={{0,28},{4,0},{8,4},{12,8},{16,12},{20,16},{24,20},{28,24},{1,29},{... | collective-permute-start | bytes 98312 | tf_op jit(solution)/shard_map/ppermute | solution.py:58
  23.0 7.0 %collective-permute-start.2 = (f32[4,2,64,16]{2,3,0,1:T(8,128)S(1)}, f32[4,2,64,16]{2,3,0,1:T(8,128)S(1)}, u32[]{:S(2)}, u32[]{:S(2)}) collective-permute-start(f32[4,2,64,16]{2,3,0,1:T(8,128)S(1)} %collective-permute-done.1), channel_id=1, source_target_pairs={{0,4},{4,8},{8,12},{12,16},{16,20},{20,24},{24,28},{28,0},{1,5},{5... | collective-permute-start | bytes 98312 | tf_op jit(solution)/shard_map/ppermute | solution.py:54
  23.5 6.5 %collective-permute-start.6 = (f32[4,2,64,16]{2,3,0,1:T(8,128)S(1)}, f32[4,2,64,16]{2,3,0,1:T(8,128)S(1)}, u32[]{:S(2)}, u32[]{:S(2)}) collective-permute-start(f32[4,2,64,16]{2,3,0,1:T(8,128)S(1)} %collective-permute-done.5), channel_id=1, source_target_pairs={{0,28},{4,0},{8,4},{12,8},{16,12},{20,16},{24,20},{28,24},{1,29},{... | collective-permute-start | bytes 98312 | tf_op jit(solution)/shard_map/ppermute | solution.py:58
  29.9 7.0 %collective-permute-start.3 = (f32[4,2,64,16]{2,3,0,1:T(8,128)S(1)}, f32[4,2,64,16]{2,3,0,1:T(8,128)S(1)}, u32[]{:S(2)}, u32[]{:S(2)}) collective-permute-start(f32[4,2,64,16]{2,3,0,1:T(8,128)S(1)} %collective-permute-done.2), channel_id=1, source_target_pairs={{0,4},{4,8},{8,12},{12,16},{16,20},{20,24},{24,28},{28,0},{1,5},{5... | collective-permute-start | bytes 98312 | tf_op jit(solution)/shard_map/ppermute | solution.py:54
  30.0 7.0 %collective-permute-start.7 = (f32[4,2,64,16]{2,3,0,1:T(8,128)S(1)}, f32[4,2,64,16]{2,3,0,1:T(8,128)S(1)}, u32[]{:S(2)}, u32[]{:S(2)}) collective-permute-start(f32[4,2,64,16]{2,3,0,1:T(8,128)S(1)} %collective-permute-done.6), channel_id=1, source_target_pairs={{0,28},{4,0},{8,4},{12,8},{16,12},{20,16},{24,20},{28,24},{1,29},{... | collective-permute-start | bytes 98312 | tf_op jit(solution)/shard_map/ppermute | solution.py:58
  36.9 7.0 %collective-permute-start.4 = (f32[4,2,64,16]{2,3,0,1:T(8,128)S(1)}, f32[4,2,64,16]{2,3,0,1:T(8,128)S(1)}, u32[]{:S(2)}, u32[]{:S(2)}) collective-permute-start(f32[4,2,64,16]{2,3,0,1:T(8,128)S(1)} %collective-permute-done.3), channel_id=1, source_target_pairs={{0,4},{4,8},{8,12},{12,16},{16,20},{20,24},{24,28},{28,0},{1,5},{5... | collective-permute-start | bytes 98312 | tf_op jit(solution)/shard_map/ppermute | solution.py:54
Sparse Core Ops, SparseCore 0:
  46.8 22.8 reduce-scatter.1
